TPU v7x, 32 devices: a whole 2x2x4 slice. The times are simulated.
32 devices in a mesh: section: 8 (over z, core), tensor: 4 (over y, x).
Axes of the slice: x: 2, y: 2, z: 4, core: 2. Of those that a mesh axis runs over, the one named last changes fastest.
Arguments:
- fwd_in: bfloat16 [8, 128, 2304], P('section', None, 'tensor'), may hold values from -6 to 6
- back_in: bfloat16 [8, 128, 2304], P('section', None, 'tensor'), may hold values from -0.59765625 to 0.59765625
- stash: bfloat16 [2, 8, 128, 2304], P(None, 'section', None, 'tensor'), may hold values from -6 to 6
- w_qkv: bfloat16 [8, 2304, 3, 4, 128], P('section', None, None, 'tensor'), may hold values from -0.125 to 0.125
- w_out: bfloat16 [8, 4, 128, 2304], P('section', 'tensor'), may hold values from -0.25 to 0.25
- norm_gain: bfloat16 [8, 2304], P('section'), may hold values from 0.25 to 1.75
- final_gain: bfloat16 [2304], replicated, may hold values from 0.25 to 1.75
- table: bfloat16 [8192, 2304], P(('section', 'tensor')), may hold values from -0.5625 to 0.5625
- ids: int32 [2, 128], replicated, may hold values from 0 to 8191
- back_ids: int32 [2, 128], replicated, may hold values from 0 to 8191
- targets: int32 [2, 128], replicated, may hold values from 0 to 8191
Outputs:
- fwd_out: bfloat16 [8, 128, 2304], P('section', None, 'tensor')
- back_out: bfloat16 [8, 128, 2304], P('section', None, 'tensor')
- table_grad: bfloat16 [8192, 2304], P(('section', 'tensor'))
- losses: float32 [2], replicated
All inputs are finite; a program needn't handle non-finite values.
Results may differ from a plain program's by a relative error of at most 0.035.
Values may be sent and summed in bfloat16 or wider, within the bound.
No kernel may reach another device: no remote copies, remote signals or barrier semaphores. Data moves between devices by JAX's collectives and lax.ppermute only.
A program may use at most 64 MiB of HBM per device.

v0:
```python
import math
import jax
import jax.numpy as jnp
from jax import lax
from jax.sharding import PartitionSpec as P

EPS = 1e-06
ATTN_CAP = 50.0
LOGIT_CAP = 30.0


def for_sending(x):

    def short(part):
        return part.astype(jnp.bfloat16) if part.dtype == jnp.float32 else part

    return jax.tree.map(short, x)


def passed_along(block, axis, distance):
    devices = range(lax.axis_size(axis))
    route = [(i - distance, i) for i in devices if i - distance in devices]
    return lax.ppermute(block, axis, route)


def broadcast(block, axis, holder):
    block = jnp.where(lax.axis_index(axis) == holder, block, jnp.zeros_like(block))
    return lax.psum(block, axis)


def widen(values):
    return jax.tree.map(
        lambda part, own: part.astype(own.dtype),
        lax.all_gather(for_sending(values), "tensor", axis=1, tiled=True),
        values,
    )


def sum_width(term):
    return lax.psum_scatter(
        term.astype(jnp.bfloat16), "tensor", scatter_dimension=1, tiled=True
    ).astype(jnp.float32)


def stat_width(values):
    return lax.psum(values, "tensor")


def sum_section(values):
    return jax.tree.map(
        lambda part: part.astype(jnp.float32), lax.psum(for_sending(values), "section")
    )


def pass_section(values, offset):
    return passed_along(values, "section", offset)


def feed(values, root):
    return broadcast(widen(values), "section", root)


def reduce_lookup(parts, width_pos, piece):
    summed = lax.psum(parts, ("section", "tensor"))
    return lax.dynamic_slice_in_dim(summed, width_pos * piece, piece, 1)


def row_scale(values):
    return lax.rsqrt(jnp.mean(values * values, axis=-1, keepdims=True) + EPS)


def attend(normed, weights):
    qkv = jnp.einsum("rd,dchk->chrk", normed, weights, preferred_element_type=jnp.float32).astype(
        jnp.bfloat16
    )
    query, keys, values = (qkv[0], qkv[1], qkv[2])
    length = normed.shape[0]
    scores = jnp.einsum(
        "hqk,hsk->hqs", query, keys, preferred_element_type=jnp.float32
    ) * query.shape[-1] ** (-0.5)
    capped = jnp.tanh(scores / ATTN_CAP)
    places = lax.iota(jnp.int32, length)
    causal = places[None, :] <= places[:, None]
    raised = jnp.where(causal[None], jnp.exp(ATTN_CAP * capped), 0.0)
    probs = (raised / jnp.sum(raised, axis=-1, keepdims=True)).astype(jnp.bfloat16)
    mixed = jnp.einsum("hqs,hsk->hqk", probs, values, preferred_element_type=jnp.float32).astype(
        jnp.bfloat16
    )
    return (query, keys, values, capped, probs, mixed)


def norm_back(xfull, xpiece, gpiece, dnorm, full_width):
    scale = row_scale(xfull)
    stat = stat_width(jnp.sum(xpiece * gpiece * dnorm, axis=1))
    return scale * gpiece * dnorm - xpiece * scale**3 * stat[:, None] / full_width


def body(
    fwd_in, back_in, stash, w_qkv, w_out, norm_gain, final_gain, table, ids, back_ids, targets
):
    section_pos = lax.axis_index("section")
    section_count = lax.axis_size("section")
    width_pos = lax.axis_index("tensor")
    width_count = lax.axis_size("tensor")
    acts = fwd_in[0]
    cots = back_in[0]
    rows, piece = acts.shape
    full_width = piece * width_count
    vocab_rows = table.shape[0]
    first_col = (section_pos * width_count + width_pos) * vocab_rows
    columns = first_col + lax.iota(jnp.int32, vocab_rows)
    emb_scale = math.sqrt(full_width)
    gain = norm_gain[0].astype(jnp.float32)
    gain_piece = lax.dynamic_slice_in_dim(gain, width_pos * piece, piece, 0)
    fgain = final_gain.astype(jnp.float32)
    fgain_piece = lax.dynamic_slice_in_dim(fgain, width_pos * piece, piece, 0)
    weights = w_qkv[0]
    outw = w_out[0]
    ticks = ids.shape[0]
    is_first = section_pos == 0
    is_last = section_pos == section_count - 1
    grad = jnp.zeros((vocab_rows, full_width), jnp.float32)
    losses = []
    previous = acts
    for tick in range(ticks):
        xfull = widen(acts).astype(jnp.float32)
        normed = (xfull * row_scale(xfull) * gain).astype(jnp.bfloat16)
        mixed = attend(normed, weights)[5]
        part = jnp.einsum("hrk,hkd->rd", mixed, outw, preferred_element_type=jnp.float32)
        outs_fwd = (acts.astype(jnp.float32) + sum_width(part)).astype(jnp.bfloat16)
        hidden = feed(outs_fwd, section_count - 1).astype(jnp.float32)
        hscale = row_scale(hidden)
        hnormed = (hidden * hscale * fgain).astype(jnp.bfloat16)
        raw = lax.dot_general(
            hnormed, table, (((1,), (1,)), ((), ())), preferred_element_type=jnp.float32
        )
        capped = jnp.tanh(raw / LOGIT_CAP)
        logits = LOGIT_CAP * capped
        raised = jnp.exp(logits)
        hit = targets[tick][:, None] == columns[None, :]
        tile_sums = stat_width(
            (jnp.sum(raised, axis=1), jnp.sum(jnp.where(hit, logits, 0.0), axis=1))
        )
        total, picked = sum_section(tile_sums)
        losses.append(jnp.mean(jnp.log(total) - picked))
        dlog = (
            (raised / total[:, None] - hit.astype(jnp.float32)) * (1.0 - capped * capped)
        ).astype(jnp.bfloat16)
        dpart = jnp.dot(dlog, table, preferred_element_type=jnp.float32)
        dhid = sum_section(sum_width(dpart))
        grad = grad + lax.dot_general(
            dlog, hnormed, (((0,), (0,)), ((), ())), preferred_element_type=jnp.float32
        )
        hpiece = lax.dynamic_slice_in_dim(hidden, width_pos * piece, piece, 1)
        cot_last = norm_back(hidden, hpiece, fgain_piece, dhid, full_width).astype(jnp.bfloat16)
        inputs_back = stash[tick, 0]
        if tick > 0:
            inputs_back = jnp.where(is_last, previous, inputs_back)
        bfull, upper = widen((inputs_back, cots))
        bfloat = bfull.astype(jnp.float32)
        bnormed = (bfloat * row_scale(bfloat) * gain).astype(jnp.bfloat16)
        query, keys, values, acapped, probs, amixed = attend(bnormed, weights)
        dmix = jnp.einsum("rd,hkd->hrk", upper, outw, preferred_element_type=jnp.float32).astype(
            jnp.bfloat16
        )
        dprob = jnp.einsum("hrk,hsk->hrs", dmix, values, preferred_element_type=jnp.float32)
        pfull = probs.astype(jnp.float32)
        dscore = pfull * (dprob - jnp.sum(dprob * pfull, axis=-1, keepdims=True))
        dlogit = (dscore * (1.0 - acapped * acapped) * query.shape[-1] ** (-0.5)).astype(
            jnp.bfloat16
        )
        dquery = jnp.einsum(
            "hqs,hsk->hqk", dlogit, keys, preferred_element_type=jnp.float32
        ).astype(jnp.bfloat16)
        dkeys = jnp.einsum(
            "hqs,hqk->hsk", dlogit, query, preferred_element_type=jnp.float32
        ).astype(jnp.bfloat16)
        dvalues = jnp.einsum(
            "hqs,hqk->hsk", probs, dmix, preferred_element_type=jnp.float32
        ).astype(jnp.bfloat16)
        stacked = jnp.stack([dquery, dkeys, dvalues])
        dterm = jnp.einsum("chrk,dchk->rd", stacked, weights, preferred_element_type=jnp.float32)
        dnorm = sum_width(dterm)
        bpiece = lax.dynamic_slice_in_dim(bfloat, width_pos * piece, piece, 1)
        dxf = norm_back(bfloat, bpiece, gain_piece, dnorm, full_width)
        outs_back = (cots.astype(jnp.float32) + dxf).astype(jnp.bfloat16)
        leaving = feed(outs_back, 0)
        back_hits = (back_ids[tick][:, None] == columns[None, :]).astype(jnp.bfloat16)
        look_grad = lax.dot_general(
            back_hits, leaving, (((0,), (0,)), ((), ())), preferred_element_type=jnp.float32
        )
        grad = grad + look_grad * emb_scale
        hits = (ids[tick][:, None] == columns[None, :]).astype(jnp.bfloat16)
        embedded = reduce_lookup(
            jnp.dot(hits, table, preferred_element_type=jnp.float32), width_pos, piece
        )
        entering = (embedded * emb_scale).astype(jnp.bfloat16)
        previous = acts
        acts = jnp.where(is_first, entering, pass_section(outs_fwd, 1))
        cots = jnp.where(is_last, cot_last, pass_section(outs_back, -1))
    return (acts[None], cots[None], grad.astype(jnp.bfloat16), jnp.stack(losses))


def solution(mesh):
    return jax.shard_map(
        body,
        mesh=mesh,
        in_specs=(
            P("section", None, "tensor"),
            P("section", None, "tensor"),
            P(None, "section", None, "tensor"),
            P("section", None, None, "tensor", None),
            P("section", "tensor", None, None),
            P("section", None),
            P(),
            P(("section", "tensor"), None),
            P(),
            P(),
            P(),
        ),
        out_specs=(
            P("section", None, "tensor"),
            P("section", None, "tensor"),
            P(("section", "tensor"), None),
            P(),
        ),
        check_vma=False,
    )
```

profile of v0, /device:TPU:0, one launch (start us, length us, event | category | flops | bytes accessed | tf_op | source)
XLA Modules:
  0.0 578.9 jit_solution(3762362679505095675)
XLA Ops:
  8.1 12.4 %all-gather = bf16[1,128,2304]{1,2,0:T(8,128)(2,1)S(1)} all-gather(bf16[1,128,576]{1,2,0:T(8,128)(2,1)} %param.11), channel_id=2, replica_groups=mesh['section'=8,'tensor'=4] {'tensor'}, dimensions={2}, use_global_device_ids=true | all-gather | bytes 737280 | tf_op jit(solution)/shard_map/all_gather | solution.py:34
  30.5 21.3 %reduce-scatter.7.cloned.1.call-done = bf16[128,576]{0,1:T(8,128)(2,1)} async-done(((bf16[128,2304]{0,1:T(8,128)(2,1)}), bf16[128,576]{0,1:T(8,128)(2,1)}) %reduce-scatter.7.cloned.1.call-update) | async-done | bytes 147472 | tf_op jit(solution)/shard_map/reduce_scatter | solution.py:40
  53.5 2.3 collective-permute-start
  55.8 113.7 %all-reduce.14.cloned.1.call-done = (f32[128,2304]{0,1:T(8,128)}, f32[128,2304]{0,1:T(8,128)}) async-done(((f32[128,2304]{0,1:T(8,128)}, f32[128,2304]{0,1:T(8,128)}), (f32[128,2304]{0,1:T(8,128)}, f32[128,2304]{0,1:T(8,128)})) %all-reduce.14.cloned.1.call-update) | async-done | bytes 2359312 | tf_op jit(solution)/shard_map/psum | solution.py:64
  171.2 11.3 %all_gather.31 = bf16[128,2304]{0,1:T(8,128)(2,1)S(1)} all-gather(bf16[128,576]{0,1:T(8,128)(2,1)S(1)} %fusion.112), channel_id=1, replica_groups=mesh['section'=8,'tensor'=4] {'tensor'}, dimensions={1}, use_global_device_ids=true | all-gather | bytes 737280 | tf_op jit(solution)/shard_map/all_gather | solution.py:34
  185.9 2.2 convolution_convert_fusion.2
  188.2 10.5 %all_gather.33 = bf16[128,2304]{0,1:T(8,128)(2,1)S(1)} all-gather(bf16[128,576]{0,1:T(8,128)(2,1)} %add_convert_fusion.1), channel_id=1, replica_groups=mesh['section'=8,'tensor'=4] {'tensor'}, dimensions={1}, use_global_device_ids=true | all-gather | bytes 737280 | tf_op jit(solution)/shard_map/all_gather | solution.py:34
  199.5 13.0 %reduce-scatter.9.cloned.1.call-done = bf16[128,576]{0,1:T(8,128)(2,1)} async-done(((bf16[128,2304]{0,1:T(8,128)(2,1)}), bf16[128,576]{0,1:T(8,128)(2,1)}) %reduce-scatter.9.cloned.1.call-update) | async-done | bytes 147472 | tf_op jit(solution)/shard_map/reduce_scatter | solution.py:40
  214.2 10.2 %all_gather.32 = bf16[128,2304]{0,1:T(8,128)(2,1)S(1)} all-gather(bf16[128,576]{0,1:T(8,128)(2,1)S(1)} %add_convert_fusion), channel_id=1, replica_groups=mesh['section'=8,'tensor'=4] {'tensor'}, dimensions={1}, use_global_device_ids=true | all-gather | bytes 737280 | tf_op jit(solution)/shard_map/all_gather | solution.py:34
  228.3 11.7 %all-gather.2 = bf16[1,128,2304]{1,2,0:T(8,128)(2,1)} all-gather(bf16[1,128,576]{1,2,0:T(8,128)(2,1)} %param.12), channel_id=4, replica_groups=mesh['section'=8,'tensor'=4] {'tensor'}, dimensions={2}, use_global_device_ids=true | all-gather | bytes 737280 | tf_op jit(solution)/shard_map/all_gather | solution.py:34
  241.2 43.7 %all-reduce.20.cloned.1.call-done = (bf16[128,2304]{0,1:T(8,128)(2,1)}, bf16[128,2304]{0,1:T(8,128)(2,1)}) async-done(((bf16[128,2304]{0,1:T(8,128)(2,1)}, bf16[128,2304]{0,1:T(8,128)(2,1)}), (bf16[128,2304]{0,1:T(8,128)(2,1)}, bf16[128,2304]{0,1:T(8,128)(2,1)})) %all-reduce.20.cloned.1.call-update) | async-done | bytes 1179664 | tf_op jit(solution)/shard_map/psum | solution.py:28
  288.9 2.3 fusion.123
  291.1 10.7 %all-reduce.3 = (bf16[128]{0:T(256)(128)(2,1)}, bf16[128]{0:T(256)(128)(2,1)}) all-reduce(f32[128]{0:T(128)} %get-tuple-element.5, f32[128]{0:T(128)} %get-tuple-element.10), channel_id=1, replica_groups=mesh['section'=8,'tensor'=4] {'tensor'}, use_global_device_ids=true, to_apply=%region_20.21 | all-reduce | flops 256 | bytes 1536 | tf_op jit(solution)/shard_map/psum | solution.py:46
  301.8 14.3 %all-reduce.5 = (bf16[128]{0:T(256)(128)(2,1)}, bf16[128]{0:T(256)(128)(2,1)}) all-reduce(bf16[128]{0:T(256)(128)(2,1)} %get-tuple-element.21, bf16[128]{0:T(256)(128)(2,1)} %get-tuple-element.20), channel_id=1, replica_groups=mesh['section'=8,'tensor'=4] {'section'}, use_global_device_ids=true, to_apply=%region_12.13 | all-reduce | flops 256 | bytes 1024 | tf_op jit(solution)/shard_map/psum | solution.py:51
  317.4 2.4 convolution_convert_fusion.1
  319.8 12.8 %all-gather.1 = bf16[1,1,128,2304]{2,3,1,0:T(8,128)(2,1)S(1)} all-gather(bf16[1,1,128,576]{2,3,1,0:T(8,128)(2,1)} %slice.70), channel_id=3, replica_groups=mesh['section'=8,'tensor'=4] {'tensor'}, dimensions={3}, use_global_device_ids=true | all-gather | bytes 737280 | tf_op jit(solution)/shard_map/all_gather | solution.py:34
  342.8 10.7 %all_gather.36 = bf16[128,2304]{0,1:T(8,128)(2,1)S(1)} all-gather(bf16[128,576]{0,1:T(8,128)(2,1)S(1)} %bitcast_select_fusion), channel_id=1, replica_groups=mesh['section'=8,'tensor'=4] {'tensor'}, dimensions={1}, use_global_device_ids=true | all-gather | bytes 737280 | tf_op jit(solution)/shard_map/all_gather | solution.py:34
  356.7 13.5 %reduce-scatter.13.cloned.1.call-done = bf16[128,576]{0,1:T(8,128)(2,1)} async-done(((bf16[128,2304]{0,1:T(8,128)(2,1)}), bf16[128,576]{0,1:T(8,128)(2,1)}) %reduce-scatter.13.cloned.1.call-update) | async-done | bytes 147472 | tf_op jit(solution)/shard_map/reduce_scatter | solution.py:40
  375.4 22.8 %reduce-scatter.15.cloned.1.call-done = bf16[128,576]{0,1:T(8,128)(2,1)} async-done(((bf16[128,2304]{0,1:T(8,128)(2,1)}), bf16[128,576]{0,1:T(8,128)(2,1)}) %reduce-scatter.15.cloned.1.call-update) | async-done | bytes 147472 | tf_op jit(solution)/shard_map/reduce_scatter | solution.py:40
  402.2 21.0 %all-reduce.18.cloned.1.call-done = (bf16[128,576]{0,1:T(8,128)(2,1)}, bf16[128,576]{0,1:T(8,128)(2,1)}) async-done(((bf16[128,576]{0,1:T(8,128)(2,1)}, bf16[128,576]{0,1:T(8,128)(2,1)}), (bf16[128,576]{0,1:T(8,128)(2,1)}, bf16[128,576]{0,1:T(8,128)(2,1)})) %all-reduce.18.cloned.1.call-update) | async-done | bytes 294928 | tf_op jit(solution)/shard_map/psum | solution.py:51
  425.2 10.5 %all-reduce.2 = (f32[128]{0:T(128)}, f32[128]{0:T(128)}) all-reduce(f32[128]{0:T(128)} %fusion.101, f32[128]{0:T(128)} %get-tuple-element.9), channel_id=1, replica_groups=mesh['section'=8,'tensor'=4] {'tensor'}, use_global_device_ids=true, to_apply=%region_31.32 | all-reduce | flops 256 | bytes 2048 | tf_op jit(solution)/shard_map/psum | solution.py:46
  439.5 3.7 collective-permute-start.1
  444.5 11.0 %all_gather.37 = bf16[128,2304]{0,1:T(8,128)(2,1)S(1)} all-gather(bf16[128,576]{0,1:T(8,128)(2,1)S(1)} %fusion.113), channel_id=1, replica_groups=mesh['section'=8,'tensor'=4] {'tensor'}, dimensions={1}, use_global_device_ids=true | all-gather | bytes 737280 | tf_op jit(solution)/shard_map/all_gather | solution.py:34
  459.9 2.3 fusion.108
  462.3 13.0 %all_gather.38 = bf16[128,2304]{0,1:T(8,128)(2,1)S(1)} all-gather(bf16[128,576]{0,1:T(8,128)(2,1)S(1)} %copy-done.18), channel_id=1, replica_groups=mesh['section'=8,'tensor'=4] {'tensor'}, dimensions={1}, use_global_device_ids=true | all-gather | bytes 737280 | tf_op jit(solution)/shard_map/all_gather | solution.py:34
  476.2 7.2 %reduce-scatter.17.cloned.1.call-done = bf16[128,576]{0,1:T(8,128)(2,1)} async-done(((bf16[128,2304]{0,1:T(8,128)(2,1)}), bf16[128,576]{0,1:T(8,128)(2,1)}) %reduce-scatter.17.cloned.1.call-update) | async-done | bytes 147472 | tf_op jit(solution)/shard_map/reduce_scatter | solution.py:40
  484.6 9.3 %all-reduce.1 = (f32[128]{0:T(128)S(1)}, f32[128]{0:T(128)S(1)}, bf16[128]{0:T(256)(128)(2,1)S(1)}, bf16[128]{0:T(256)(128)(2,1)S(1)}) all-reduce(f32[128]{0:T(128)S(1)} %fusion.105, f32[128]{0:T(128)S(1)} %copy-done.55, f32[128]{0:T(128)S(1)} %copy-done.63, f32[128]{0:T(128)S(1)} %copy-done.62), channel_id=1, replica_groups=mesh['section'=8,'tensor'=4] {'tensor'}, use_global_device_ids=true, to_apply=%region_37.38 | all-reduce | flops 512 | bytes 3584 | tf_op jit(solution)/shard_map/psum | solution.py:46
  495.1 10.6 %all_gather.39 = bf16[128,2304]{0,1:T(8,128)(2,1)S(1)} all-gather(bf16[128,576]{0,1:T(8,128)(2,1)S(1)} %fusion.104), channel_id=1, replica_groups=mesh['section'=8,'tensor'=4] {'tensor'}, dimensions={1}, use_global_device_ids=true | all-gather | bytes 737280 | tf_op jit(solution)/shard_map/all_gather | solution.py:34
  506.7 2.3 fusion.109
  510.3 17.9 %all-reduce.4 = (bf16[128]{0:T(256)(128)(2,1)S(1)}, bf16[128]{0:T(256)(128)(2,1)S(1)}) all-reduce(bf16[128]{0:T(256)(128)(2,1)S(1)} %get-tuple-element.16, bf16[128]{0:T(256)(128)(2,1)S(1)} %get-tuple-element.17), channel_id=1, replica_groups=mesh['section'=8,'tensor'=4] {'section'}, use_global_device_ids=true, to_apply=%region_46.47 | all-reduce | flops 256 | bytes 1024 | tf_op jit(solution)/shard_map/psum | solution.py:51
  533.0 33.5 %all-reduce.16.cloned.1.call-done = (bf16[128,2304]{0,1:T(8,128)(2,1)}, bf16[128,2304]{0,1:T(8,128)(2,1)}) async-done(((bf16[128,2304]{0,1:T(8,128)(2,1)}, bf16[128,2304]{0,1:T(8,128)(2,1)}), (bf16[128,2304]{0,1:T(8,128)(2,1)}, bf16[128,2304]{0,1:T(8,128)(2,1)})) %all-reduce.16.cloned.1.call-update) | async-done | bytes 1179664 | tf_op jit(solution)/shard_map/psum | solution.py:28
  566.5 3.2 fusion.2
  (237 shorter events, 74.0 us)
Async XLA Ops:
  8.0 43.8 %reduce-scatter.7.cloned.1.call-start = ((), (), s32[]{:S(2)}) async-start(), calls=%async_computation.6 | async-start | bytes 737280 | tf_op jit(solution)/shard_map/reduce_scatter | solution.py:40
  26.3 143.2 %all-reduce.14.cloned.1.call-start = ((), (), s32[]{:S(2)}) async-start(), calls=%async_computation.12 | async-start | bytes 4718592 | tf_op jit(solution)/shard_map/psum | solution.py:64
  26.4 310.4 %copy-start.30 = (s32[256]{0:T(256)}, s32[256]{0:T(256)S(1)}, u32[]{:S(2)}) copy-start(s32[256]{0:T(256)S(1)} %iota_add_fusion) | copy-start | bytes 3076
  30.5 182.1 %reduce-scatter.9.cloned.1.call-start = ((), (), s32[]{:S(2)}) async-start(), calls=%async_computation.7 | async-start | bytes 737280 | tf_op jit(solution)/shard_map/reduce_scatter | solution.py:40
  53.5 116.0 %collective-permute-start = (bf16[128,576]{0,1:T(8,128)(2,1)}, bf16[128,576]{0,1:T(8,128)(2,1)}, u32[]{:S(2)}, u32[]{:S(2)}) collective-permute-start(bf16[128,576]{0,1:T(8,128)(2,1)} %add_convert_fusion.1), channel_id=1, source_target_pairs={{0,4},{4,8},{8,12},{12,16},{16,20},{20,24},{24,28},{1,5},{5,9},{9,... | collective-permute-start | bytes 442376 | tf_op jit(solution)/shard_map/ppermute | solution.py:23
  188.1 96.8 %all-reduce.20.cloned.1.call-start = ((), (), s32[]{:S(2)}) async-start(), calls=%async_computation.15 | async-start | bytes 2359296 | tf_op jit(solution)/shard_map/psum | solution.py:28
  225.3 131.3 %reduce-scatter.11.cloned.1.call-start = ((), (), s32[]{:S(2)}) async-start(), calls=%async_computation.8 | async-start | bytes 737280 | tf_op jit(solution)/shard_map/reduce_scatter | solution.py:40
  319.8 50.3 %reduce-scatter.13.cloned.1.call-start = ((), (), s32[]{:S(2)}) async-start(), calls=%async_computation.9 | async-start | bytes 737280 | tf_op jit(solution)/shard_map/reduce_scatter | solution.py:40
  338.7 59.5 %reduce-scatter.15.cloned.1.call-start = ((), (), s32[]{:S(2)}) async-start(), calls=%async_computation.10 | async-start | bytes 737280 | tf_op jit(solution)/shard_map/reduce_scatter | solution.py:40
  342.7 80.5 %all-reduce.18.cloned.1.call-start = ((), (), s32[]{:S(2)}) async-start(), calls=%async_computation.14 | async-start | bytes 589824 | tf_op jit(solution)/shard_map/psum | solution.py:51
  370.2 113.2 %reduce-scatter.17.cloned.1.call-start = ((), (), s32[]{:S(2)}) async-start(), calls=%async_computation.11 | async-start | bytes 737280 | tf_op jit(solution)/shard_map/reduce_scatter | solution.py:40
  373.3 26.6 %copy-start.8 = (bf16[128,2304]{0,1:T(8,128)(2,1)S(1)}, bf16[128,2304]{0,1:T(8,128)(2,1)}, u32[]{:S(2)}) copy-start(bf16[128,2304]{0,1:T(8,128)(2,1)} %get-tuple-element.30) | copy-start | bytes 1769476
  374.2 69.0 %copy-start.33 = (f32[576]{0:T(1024)}, f32[576]{0:T(1024)S(1)}, u32[]{:S(2)}) copy-start(f32[576]{0:T(1024)S(1)} %dynamic_slice.28) | copy-start | bytes 6916
  375.3 25.8 %copy-start.6 = (bf16[128,2304]{0,1:T(8,128)(2,1)S(1)}, bf16[128,2304]{0,1:T(8,128)(2,1)}, u32[]{:S(2)}) copy-start(bf16[128,2304]{0,1:T(8,128)(2,1)} %get-tuple-element.31) | copy-start | bytes 1769476
  401.1 34.5 %copy-start.59 = (f32[128]{0:T(128)S(1)}, f32[128]{0:T(128)}, u32[]{:S(2)}) copy-start(f32[128]{0:T(128)} %copy-done.58) | copy-start | bytes 1540
  402.2 41.0 %copy-start.47 = (f32[128]{0:T(128)S(1)}, f32[128]{0:T(128)}, u32[]{:S(2)}) copy-start(f32[128]{0:T(128)} %copy-done.46) | copy-start | bytes 1540
  436.9 6.3 %collective-permute-start.2 = (bf16[128,576]{0,1:T(8,128)(2,1)S(1)}, bf16[128,576]{0,1:T(8,128)(2,1)S(1)}, u32[]{:S(2)}, u32[]{:S(2)}) collective-permute-start(bf16[128,576]{0,1:T(8,128)(2,1)S(1)} %fusion.100), channel_id=1, source_target_pairs={{4,0},{8,4},{12,8},{16,12},{20,16},{24,20},{28,24},{5,1},{9,5},{13... | collective-permute-start | bytes 442376 | tf_op jit(solution)/shard_map/ppermute | solution.py:23
  439.5 18.7 %collective-permute-start.1 = (bf16[128,576]{0,1:T(8,128)(2,1)}, bf16[128,576]{0,1:T(8,128)(2,1)}, u32[]{:S(2)}, u32[]{:S(2)}) collective-permute-start(bf16[128,576]{0,1:T(8,128)(2,1)} %copy-done.15), channel_id=1, source_target_pairs={{0,4},{4,8},{8,12},{12,16},{16,20},{20,24},{24,28},{1,5},{5,9},{9,... | collective-permute-start | bytes 442376 | tf_op jit(solution)/shard_map/ppermute | solution.py:23
  458.1 108.4 %all-reduce.16.cloned.1.call-start = ((), (), s32[]{:S(2)}) async-start(), calls=%async_computation.13 | async-start | bytes 2359296 | tf_op jit(solution)/shard_map/psum | solution.py:28
  462.2 22.3 %copy-start.55 = (f32[128]{0:T(128)S(1)}, f32[128]{0:T(128)}, u32[]{:S(2)}) copy-start(f32[128]{0:T(128)} %get-tuple-element.8) | copy-start | bytes 1540
  462.2 22.3 %copy-start.62 = (f32[128]{0:T(128)S(1)}, f32[128]{0:T(128)}, u32[]{:S(2)}) copy-start(f32[128]{0:T(128)} %get-tuple-element.4) | copy-start | bytes 1540
  462.2 22.3 %copy-start.63 = (f32[128]{0:T(128)S(1)}, f32[128]{0:T(128)}, u32[]{:S(2)}) copy-start(f32[128]{0:T(128)} %get-tuple-element.11) | copy-start | bytes 1540
  462.2 31.6 %copy-start.12 = (bf16[128,576]{0,1:T(8,128)(2,1)S(1)}, bf16[128,576]{0,1:T(8,128)(2,1)}, u32[]{:S(2)}) copy-start(bf16[128,576]{0,1:T(8,128)(2,1)} %copy-done.11) | copy-start | bytes 442372
  462.2 31.6 %copy-start.57 = (f32[128]{0:T(128)S(1)}, f32[128]{0:T(128)}, u32[]{:S(2)}) copy-start(f32[128]{0:T(128)} %copy-done.56) | copy-start | bytes 1540
  462.3 31.6 %copy-start.64 = (f32[128]{0:T(128)S(1)}, f32[128]{0:T(128)}, u32[]{:S(2)}) copy-start(f32[128]{0:T(128)} %get-tuple-element.40) | copy-start | bytes 1540
  506.7 22.1 %copy-start.66 = (bf16[128]{0:T(256)(128)(2,1)S(1)}, bf16[128]{0:T(256)(128)(2,1)}, u32[]{:S(2)}) copy-start(bf16[128]{0:T(256)(128)(2,1)} %get-tuple-element.25) | copy-start | bytes 772
  506.7 24.5 %copy-start.16 = (bf16[128,576]{0,1:T(8,128)(2,1)S(1)}, bf16[128,576]{0,1:T(8,128)(2,1)}, u32[]{:S(2)}) copy-start(bf16[128,576]{0,1:T(8,128)(2,1)} %get-tuple-element.28) | copy-start | bytes 442372
  506.7 24.5 %copy-start.34 = (f32[576]{0:T(1024)S(1)}, f32[576]{0:T(1024)}, u32[]{:S(2)}) copy-start(f32[576]{0:T(1024)} %copy-done.33) | copy-start | bytes 6916
  506.7 24.5 %copy-start.45 = (f32[128]{0:T(128)S(1)}, f32[128]{0:T(128)}, u32[]{:S(2)}) copy-start(f32[128]{0:T(128)} %copy-done.43) | copy-start | bytes 1540
  506.7 24.5 %copy-start.60 = (f32[128]{0:T(128)S(1)}, f32[128]{0:T(128)}, u32[]{:S(2)}) copy-start(f32[128]{0:T(128)} %get-tuple-element.38) | copy-start | bytes 1540
  506.7 59.8 %copy-start.54 = (s32[128]{0:T(128)S(1)}, s32[128]{0:T(128)}, u32[]{:S(2)}) copy-start(s32[128]{0:T(128)} %get-tuple-element.33) | copy-start | bytes 1540
  509.0 22.2 %collective-permute-start.3 = (bf16[128,576]{0,1:T(8,128)(2,1)S(1)}, bf16[128,576]{0,1:T(8,128)(2,1)S(1)}, u32[]{:S(2)}, u32[]{:S(2)}) collective-permute-start(bf16[128,576]{0,1:T(8,128)(2,1)S(1)} %fusion.104), channel_id=1, source_target_pairs={{4,0},{8,4},{12,8},{16,12},{20,16},{24,20},{28,24},{5,1},{9,5},{13... | collective-permute-start | bytes 442376 | tf_op jit(solution)/shard_map/ppermute | solution.py:23
  (50 other events, 195.4 us)
Sparse Core Ops, SparseCore 0:
  26.4 25.3 reduce-scatter.6
  188.2 24.2 reduce-scatter.8
  319.9 22.2 reduce-scatter.10
  344.9 25.1 reduce-scatter.12
  373.1 25.1 reduce-scatter.14
  458.2 25.0 reduce-scatter.16
Sparse Core Ops, SparseCore 1:
  34.0 135.5 all-reduce.13
  225.4 59.5 all-reduce.19
  370.2 52.9 all-reduce.17
  506.7 59.8 all-reduce.15
where the time goes:
time: 580 us; the launch traced here: 579 us
  waiting for transfers between devices  290 us (50%)
  blocking collectives  177 us (31%)
  matrix products  41.2 us (7%)
  other arithmetic  33.3 us (6%)
  between operations  17.7 us (3%)
  local copies, waits for them, and re-layouts  10.9 us (2%)
  starting transfers between devices  8.97 us (2%)
    all_gather x10, blocking collectives, widen(): lax.all_gather(for_sending(values), 'tensor', axis=1, tiled=True)  114 us
    psum x1, waiting for transfers between devices, reduce_lookup(): summed = lax.psum(parts, ('section', 'tensor'))  114 us
    reduce_scatter x6, waiting for transfers between devices, sum_width(): lax.psum_scatter(term.astype(jnp.bfloat16), 'tensor', scatter_dimension=1...  77.8 us
    psum x2, waiting for transfers between devices, broadcast(): return lax.psum(block, axis)  77.3 us
    psum x2, blocking collectives, sum_section(): lax.psum(for_sending(values), 'section')  32.2 us
    psum x3, blocking collectives, stat_width(): return lax.psum(values, 'tensor')  30.4 us
    psum x1, waiting for transfers between devices, sum_section(): lax.psum(for_sending(values), 'section')  21 us
  transfers between devices with their start and end apart: 14, of which 9 were waited for; matrix products, arithmetic and copies ran while one was open for 8% of the time, Pallas kernels for 0%

commit v1 on v0

--- a/solution.py
+++ b/solution.py
@@ -9,6 +9,12 @@
 LOGIT_CAP = 30.0
 
 
+def advance_the_slices(mesh_dim, peer_axis, tile_in):
+    for kk in (peer_axis, mesh_dim):
+        tile_in = lax.psum(tile_in, axis_name=kk)
+    return tile_in
+
+
 def for_sending(x):
 
     def short(part):
@@ -61,7 +67,7 @@
 
 
 def reduce_lookup(parts, width_pos, piece):
-    summed = lax.psum(parts, ("section", "tensor"))
+    summed = advance_the_slices("section", "tensor", tile_in=parts)
     return lax.dynamic_slice_in_dim(summed, width_pos * piece, piece, 1)
 
 

time: 580 us -> 630 us (1.086)
  waiting for transfers between devices: 290 us -> 338 us
    psum x1, waiting for transfers between devices: 21 us -> 51.6 us  [sum_section(): lax.psum(for_sending(values), 'section')]
    psum x1 -> x2, waiting for transfers between devices: 114 us -> 123 us  [advance_the_slices(): tile_in = lax.psum(tile_in, axis_name=kk)]
    reduce_scatter x6, waiting for transfers between devices: 77.8 us -> 86.1 us  [sum_width(): lax.psum_scatter(term.astype(jnp.bfloat16), 'tensor', scatter_dimension=1...]
  transfers between devices with their start and end apart: 14 -> 15, of which waited for: 9 -> 11; matrix products, arithmetic and copies ran while one was open for 8% -> 8% of each run, Pallas kernels for 0% -> 0%
where the time goes in v1:
time: 630 us; the launch traced here: 629 us
  waiting for transfers between devices  338 us (54%)
  blocking collectives  178 us (28%)
  matrix products  43.3 us (7%)
  other arithmetic  32.7 us (5%)
  between operations  16 us (3%)
  local copies, waits for them, and re-layouts  11.6 us (2%)
  starting transfers between devices  8.99 us (1%)
    psum x2, waiting for transfers between devices, advance_the_slices(): tile_in = lax.psum(tile_in, axis_name=kk)  123 us
    all_gather x10, blocking collectives, widen(): lax.all_gather(for_sending(values), 'tensor', axis=1, tiled=True)  115 us
    reduce_scatter x6, waiting for transfers between devices, sum_width(): lax.psum_scatter(term.astype(jnp.bfloat16), 'tensor', scatter_dimension=1...  86.1 us
    psum x2, waiting for transfers between devices, broadcast(): return lax.psum(block, axis)  77.1 us
    psum x1, waiting for transfers between devices, sum_section(): lax.psum(for_sending(values), 'section')  51.6 us
    psum x2, blocking collectives, sum_section(): lax.psum(for_sending(values), 'section')  32.4 us
    psum x3, blocking collectives, stat_width(): return lax.psum(values, 'tensor')  30.3 us
  transfers between devices with their start and end apart: 15, of which 11 were waited for; matrix products, arithmetic and copies ran while one was open for 8% of the time, Pallas kernels for 0%

profile of v1, /device:TPU:0, one launch (start us, length us, event | category | flops | bytes accessed | tf_op | source)
XLA Modules:
  0.0 628.7 jit_solution(16586042823150670020)
XLA Ops:
  8.1 3.0 fusion.124
  13.7 14.8 %all-gather = bf16[1,128,2304]{1,2,0:T(8,128)(2,1)S(1)} all-gather(bf16[1,128,576]{1,2,0:T(8,128)(2,1)S(1)} %copy-done.10), channel_id=2, replica_groups=mesh['section'=8,'tensor'=4] {'tensor'}, dimensions={2}, use_global_device_ids=true | all-gather | bytes 737280 | tf_op jit(solution)/shard_map/all_gather | solution.py:40
  34.2 58.0 %all-reduce.18.cloned.1.call-done = (f32[128,2304]{0,1:T(8,128)}, f32[128,2304]{0,1:T(8,128)}) async-done(((f32[128,2304]{0,1:T(8,128)}, f32[128,2304]{0,1:T(8,128)}), (f32[128,2304]{0,1:T(8,128)}, f32[128,2304]{0,1:T(8,128)})) %all-reduce.18.cloned.1.call-update) | async-done | bytes 2359312 | tf_op jit(solution)/shard_map/psum | solution.py:14
  92.2 28.2 %reduce-scatter.7.cloned.1.call-done = bf16[128,576]{0,1:T(8,128)(2,1)} async-done(((bf16[128,2304]{0,1:T(8,128)(2,1)}), bf16[128,576]{0,1:T(8,128)(2,1)}) %reduce-scatter.7.cloned.1.call-update) | async-done | bytes 147472 | tf_op jit(solution)/shard_map/reduce_scatter | solution.py:46
  122.1 2.3 collective-permute-start
  125.0 64.8 %all-reduce.16.cloned.1.call-done = (f32[128,2304]{0,1:T(8,128)}, f32[128,2304]{0,1:T(8,128)}) async-done(((f32[128,2304]{0,1:T(8,128)}, f32[128,2304]{0,1:T(8,128)}), (f32[128,2304]{0,1:T(8,128)}, f32[128,2304]{0,1:T(8,128)})) %all-reduce.16.cloned.1.call-update) | async-done | bytes 2359312 | tf_op jit(solution)/shard_map/psum | solution.py:14
  191.6 11.0 %all_gather.31 = bf16[128,2304]{0,1:T(8,128)(2,1)S(1)} all-gather(bf16[128,576]{0,1:T(8,128)(2,1)S(1)} %fusion.112), channel_id=1, replica_groups=mesh['section'=8,'tensor'=4] {'tensor'}, dimensions={1}, use_global_device_ids=true | all-gather | bytes 737280 | tf_op jit(solution)/shard_map/all_gather | solution.py:40
  208.2 10.2 %all_gather.33 = bf16[128,2304]{0,1:T(8,128)(2,1)S(1)} all-gather(bf16[128,576]{0,1:T(8,128)(2,1)} %add_convert_fusion.1), channel_id=1, replica_groups=mesh['section'=8,'tensor'=4] {'tensor'}, dimensions={1}, use_global_device_ids=true | all-gather | bytes 737280 | tf_op jit(solution)/shard_map/all_gather | solution.py:40
  219.3 13.0 %reduce-scatter.9.cloned.1.call-done = bf16[128,576]{0,1:T(8,128)(2,1)} async-done(((bf16[128,2304]{0,1:T(8,128)(2,1)}), bf16[128,576]{0,1:T(8,128)(2,1)}) %reduce-scatter.9.cloned.1.call-update) | async-done | bytes 147472 | tf_op jit(solution)/shard_map/reduce_scatter | solution.py:46
  234.0 10.2 %all_gather.32 = bf16[128,2304]{0,1:T(8,128)(2,1)S(1)} all-gather(bf16[128,576]{0,1:T(8,128)(2,1)S(1)} %add_convert_fusion), channel_id=1, replica_groups=mesh['section'=8,'tensor'=4] {'tensor'}, dimensions={1}, use_global_device_ids=true | all-gather | bytes 737280 | tf_op jit(solution)/shard_map/all_gather | solution.py:40
  248.0 11.7 %all-gather.2 = bf16[1,128,2304]{1,2,0:T(8,128)(2,1)} all-gather(bf16[1,128,576]{1,2,0:T(8,128)(2,1)} %param.12), channel_id=4, replica_groups=mesh['section'=8,'tensor'=4] {'tensor'}, dimensions={2}, use_global_device_ids=true | all-gather | bytes 737280 | tf_op jit(solution)/shard_map/all_gather | solution.py:40
  260.9 43.7 %all-reduce.24.cloned.1.call-done = (bf16[128,2304]{0,1:T(8,128)(2,1)}, bf16[128,2304]{0,1:T(8,128)(2,1)}) async-done(((bf16[128,2304]{0,1:T(8,128)(2,1)}, bf16[128,2304]{0,1:T(8,128)(2,1)}), (bf16[128,2304]{0,1:T(8,128)(2,1)}, bf16[128,2304]{0,1:T(8,128)(2,1)})) %all-reduce.24.cloned.1.call-update) | async-done | bytes 1179664 | tf_op jit(solution)/shard_map/psum | solution.py:34
  310.9 10.6 %all-reduce.3 = (bf16[128]{0:T(256)(128)(2,1)}, bf16[128]{0:T(256)(128)(2,1)}) all-reduce(f32[128]{0:T(128)} %get-tuple-element.5, f32[128]{0:T(128)} %get-tuple-element.10), channel_id=1, replica_groups=mesh['section'=8,'tensor'=4] {'tensor'}, use_global_device_ids=true, to_apply=%region_22.23 | all-reduce | flops 256 | bytes 1536 | tf_op jit(solution)/shard_map/psum | solution.py:52
  321.5 14.4 %all-reduce.6 = (bf16[128]{0:T(256)(128)(2,1)}, bf16[128]{0:T(256)(128)(2,1)}) all-reduce(bf16[128]{0:T(256)(128)(2,1)} %get-tuple-element.21, bf16[128]{0:T(256)(128)(2,1)} %get-tuple-element.20), channel_id=1, replica_groups=mesh['section'=8,'tensor'=4] {'section'}, use_global_device_ids=true, to_apply=%region_14.15 | all-reduce | flops 256 | bytes 1024 | tf_op jit(solution)/shard_map/psum | solution.py:57
  337.0 2.4 convolution_convert_fusion.1
  339.5 12.8 %all-gather.1 = bf16[1,1,128,2304]{2,3,1,0:T(8,128)(2,1)S(1)} all-gather(bf16[1,1,128,576]{2,3,1,0:T(8,128)(2,1)} %slice.70), channel_id=3, replica_groups=mesh['section'=8,'tensor'=4] {'tensor'}, dimensions={3}, use_global_device_ids=true | all-gather | bytes 737280 | tf_op jit(solution)/shard_map/all_gather | solution.py:40
  362.5 9.7 %all_gather.36 = bf16[128,2304]{0,1:T(8,128)(2,1)S(1)} all-gather(bf16[128,576]{0,1:T(8,128)(2,1)S(1)} %bitcast_select_fusion), channel_id=1, replica_groups=mesh['section'=8,'tensor'=4] {'tensor'}, dimensions={1}, use_global_device_ids=true | all-gather | bytes 737280 | tf_op jit(solution)/shard_map/all_gather | solution.py:40
  375.3 14.9 %reduce-scatter.13.cloned.1.call-done = bf16[128,576]{0,1:T(8,128)(2,1)} async-done(((bf16[128,2304]{0,1:T(8,128)(2,1)}), bf16[128,576]{0,1:T(8,128)(2,1)}) %reduce-scatter.13.cloned.1.call-update) | async-done | bytes 147472 | tf_op jit(solution)/shard_map/reduce_scatter | solution.py:46
  395.6 22.8 %reduce-scatter.15.cloned.1.call-done = bf16[128,576]{0,1:T(8,128)(2,1)} async-done(((bf16[128,2304]{0,1:T(8,128)(2,1)}), bf16[128,576]{0,1:T(8,128)(2,1)}) %reduce-scatter.15.cloned.1.call-update) | async-done | bytes 147472 | tf_op jit(solution)/shard_map/reduce_scatter | solution.py:46
  422.4 51.6 %all-reduce.22.cloned.1.call-done = (bf16[128,576]{0,1:T(8,128)(2,1)}, bf16[128,576]{0,1:T(8,128)(2,1)}) async-done(((bf16[128,576]{0,1:T(8,128)(2,1)}, bf16[128,576]{0,1:T(8,128)(2,1)}), (bf16[128,576]{0,1:T(8,128)(2,1)}, bf16[128,576]{0,1:T(8,128)(2,1)})) %all-reduce.22.cloned.1.call-update) | async-done | bytes 294928 | tf_op jit(solution)/shard_map/psum | solution.py:57
  475.8 10.5 %all-reduce.2 = (f32[128]{0:T(128)}, f32[128]{0:T(128)}) all-reduce(f32[128]{0:T(128)} %fusion.101, f32[128]{0:T(128)} %get-tuple-element.9), channel_id=1, replica_groups=mesh['section'=8,'tensor'=4] {'tensor'}, use_global_device_ids=true, to_apply=%region_33.34 | all-reduce | flops 256 | bytes 2048 | tf_op jit(solution)/shard_map/psum | solution.py:52
  490.1 3.7 collective-permute-start.1
  495.1 11.0 %all_gather.37 = bf16[128,2304]{0,1:T(8,128)(2,1)S(1)} all-gather(bf16[128,576]{0,1:T(8,128)(2,1)S(1)} %fusion.113), channel_id=1, replica_groups=mesh['section'=8,'tensor'=4] {'tensor'}, dimensions={1}, use_global_device_ids=true | all-gather | bytes 737280 | tf_op jit(solution)/shard_map/all_gather | solution.py:40
  510.5 2.3 fusion.108
  512.9 13.0 %all_gather.38 = bf16[128,2304]{0,1:T(8,128)(2,1)S(1)} all-gather(bf16[128,576]{0,1:T(8,128)(2,1)S(1)} %copy-done.19), channel_id=1, replica_groups=mesh['section'=8,'tensor'=4] {'tensor'}, dimensions={1}, use_global_device_ids=true | all-gather | bytes 737280 | tf_op jit(solution)/shard_map/all_gather | solution.py:40
  526.7 7.2 %reduce-scatter.17.cloned.1.call-done = bf16[128,576]{0,1:T(8,128)(2,1)} async-done(((bf16[128,2304]{0,1:T(8,128)(2,1)}), bf16[128,576]{0,1:T(8,128)(2,1)}) %reduce-scatter.17.cloned.1.call-update) | async-done | bytes 147472 | tf_op jit(solution)/shard_map/reduce_scatter | solution.py:46
  535.2 9.3 %all-reduce.1 = (f32[128]{0:T(128)S(1)}, f32[128]{0:T(128)S(1)}, bf16[128]{0:T(256)(128)(2,1)S(1)}, bf16[128]{0:T(256)(128)(2,1)S(1)}) all-reduce(f32[128]{0:T(128)S(1)} %fusion.105, f32[128]{0:T(128)S(1)} %copy-done.57, f32[128]{0:T(128)S(1)} %copy-done.65, f32[128]{0:T(128)S(1)} %copy-done.64), channel_id=1, replica_groups=mesh['section'=8,'tensor'=4] {'tensor'}, use_global_device_ids=true, to_apply=%region_39.40 | all-reduce | flops 512 | bytes 3584 | tf_op jit(solution)/shard_map/psum | solution.py:52
  545.7 10.6 %all_gather.39 = bf16[128,2304]{0,1:T(8,128)(2,1)S(1)} all-gather(bf16[128,576]{0,1:T(8,128)(2,1)S(1)} %fusion.104), channel_id=1, replica_groups=mesh['section'=8,'tensor'=4] {'tensor'}, dimensions={1}, use_global_device_ids=true | all-gather | bytes 737280 | tf_op jit(solution)/shard_map/all_gather | solution.py:40
  557.3 2.3 fusion.109
  560.9 18.0 %all-reduce.5 = (bf16[128]{0:T(256)(128)(2,1)S(1)}, bf16[128]{0:T(256)(128)(2,1)S(1)}) all-reduce(bf16[128]{0:T(256)(128)(2,1)S(1)} %get-tuple-element.16, bf16[128]{0:T(256)(128)(2,1)S(1)} %get-tuple-element.17), channel_id=1, replica_groups=mesh['section'=8,'tensor'=4] {'section'}, use_global_device_ids=true, to_apply=%region_48.49 | all-reduce | flops 256 | bytes 1024 | tf_op jit(solution)/shard_map/psum | solution.py:57
  583.9 33.4 %all-reduce.20.cloned.1.call-done = (bf16[128,2304]{0,1:T(8,128)(2,1)}, bf16[128,2304]{0,1:T(8,128)(2,1)}) async-done(((bf16[128,2304]{0,1:T(8,128)(2,1)}, bf16[128,2304]{0,1:T(8,128)(2,1)}), (bf16[128,2304]{0,1:T(8,128)(2,1)}, bf16[128,2304]{0,1:T(8,128)(2,1)})) %all-reduce.20.cloned.1.call-update) | async-done | bytes 1179664 | tf_op jit(solution)/shard_map/psum | solution.py:34
  617.4 3.2 fusion.2
  (244 shorter events, 78.3 us)
Async XLA Ops:
  7.2 85.0 %all-reduce.18.cloned.1.call-start = ((), (), s32[]{:S(2)}) async-start(), calls=%async_computation.13 | async-start | bytes 4718592 | tf_op jit(solution)/shard_map/psum | solution.py:14
  7.2 349.1 %copy-start.31 = (s32[256]{0:T(256)}, s32[256]{0:T(256)S(1)}, u32[]{:S(2)}) copy-start(s32[256]{0:T(256)S(1)} %iota_add_fusion) | copy-start | bytes 3076
  12.8 107.6 %reduce-scatter.7.cloned.1.call-start = ((), (), s32[]{:S(2)}) async-start(), calls=%async_computation.6 | async-start | bytes 737280 | tf_op jit(solution)/shard_map/reduce_scatter | solution.py:46
  34.1 155.7 %all-reduce.16.cloned.1.call-start = ((), (), s32[]{:S(2)}) async-start(), calls=%async_computation.12 | async-start | bytes 4718592 | tf_op jit(solution)/shard_map/psum | solution.py:14
  92.2 140.1 %reduce-scatter.9.cloned.1.call-start = ((), (), s32[]{:S(2)}) async-start(), calls=%async_computation.7 | async-start | bytes 737280 | tf_op jit(solution)/shard_map/reduce_scatter | solution.py:46
  122.1 3.0 collective-permute-start
  208.2 96.5 %all-reduce.24.cloned.1.call-start = ((), (), s32[]{:S(2)}) async-start(), calls=%async_computation.16 | async-start | bytes 2359296 | tf_op jit(solution)/shard_map/psum | solution.py:34
  245.0 130.3 %reduce-scatter.11.cloned.1.call-start = ((), (), s32[]{:S(2)}) async-start(), calls=%async_computation.8 | async-start | bytes 737280 | tf_op jit(solution)/shard_map/reduce_scatter | solution.py:46
  339.5 50.8 %reduce-scatter.13.cloned.1.call-start = ((), (), s32[]{:S(2)}) async-start(), calls=%async_computation.9 | async-start | bytes 737280 | tf_op jit(solution)/shard_map/reduce_scatter | solution.py:46
  358.4 60.1 %reduce-scatter.15.cloned.1.call-start = ((), (), s32[]{:S(2)}) async-start(), calls=%async_computation.10 | async-start | bytes 737280 | tf_op jit(solution)/shard_map/reduce_scatter | solution.py:46
  362.4 111.6 %all-reduce.22.cloned.1.call-start = ((), (), s32[]{:S(2)}) async-start(), calls=%async_computation.15 | async-start | bytes 589824 | tf_op jit(solution)/shard_map/psum | solution.py:57
  390.2 143.7 %reduce-scatter.17.cloned.1.call-start = ((), (), s32[]{:S(2)}) async-start(), calls=%async_computation.11 | async-start | bytes 737280 | tf_op jit(solution)/shard_map/reduce_scatter | solution.py:46
  393.5 26.6 %copy-start.8 = (bf16[128,2304]{0,1:T(8,128)(2,1)S(1)}, bf16[128,2304]{0,1:T(8,128)(2,1)}, u32[]{:S(2)}) copy-start(bf16[128,2304]{0,1:T(8,128)(2,1)} %get-tuple-element.32) | copy-start | bytes 1769476
  394.4 99.5 %copy-start.34 = (f32[576]{0:T(1024)}, f32[576]{0:T(1024)S(1)}, u32[]{:S(2)}) copy-start(f32[576]{0:T(1024)S(1)} %dynamic_slice.28) | copy-start | bytes 6916
  395.5 25.8 %copy-start.6 = (bf16[128,2304]{0,1:T(8,128)(2,1)S(1)}, bf16[128,2304]{0,1:T(8,128)(2,1)}, u32[]{:S(2)}) copy-start(bf16[128,2304]{0,1:T(8,128)(2,1)} %get-tuple-element.33) | copy-start | bytes 1769476
  421.3 65.0 %copy-start.61 = (f32[128]{0:T(128)S(1)}, f32[128]{0:T(128)}, u32[]{:S(2)}) copy-start(f32[128]{0:T(128)} %copy-done.60) | copy-start | bytes 1540
  422.4 71.5 %copy-start.49 = (f32[128]{0:T(128)S(1)}, f32[128]{0:T(128)}, u32[]{:S(2)}) copy-start(f32[128]{0:T(128)} %copy-done.48) | copy-start | bytes 1540
  487.6 6.3 collective-permute-start.2
  490.1 18.6 %collective-permute-start.1 = (bf16[128,576]{0,1:T(8,128)(2,1)}, bf16[128,576]{0,1:T(8,128)(2,1)}, u32[]{:S(2)}, u32[]{:S(2)}) collective-permute-start(bf16[128,576]{0,1:T(8,128)(2,1)} %copy-done.16), channel_id=1, source_target_pairs={{0,4},{4,8},{8,12},{12,16},{16,20},{20,24},{24,28},{1,5},{5,9},{9,... | collective-permute-start | bytes 442376 | tf_op jit(solution)/shard_map/ppermute | solution.py:29
  508.7 108.6 %all-reduce.20.cloned.1.call-start = ((), (), s32[]{:S(2)}) async-start(), calls=%async_computation.14 | async-start | bytes 2359296 | tf_op jit(solution)/shard_map/psum | solution.py:34
  512.8 22.3 %copy-start.57 = (f32[128]{0:T(128)S(1)}, f32[128]{0:T(128)}, u32[]{:S(2)}) copy-start(f32[128]{0:T(128)} %get-tuple-element.8) | copy-start | bytes 1540
  512.8 22.3 %copy-start.64 = (f32[128]{0:T(128)S(1)}, f32[128]{0:T(128)}, u32[]{:S(2)}) copy-start(f32[128]{0:T(128)} %get-tuple-element.4) | copy-start | bytes 1540
  512.8 22.3 %copy-start.65 = (f32[128]{0:T(128)S(1)}, f32[128]{0:T(128)}, u32[]{:S(2)}) copy-start(f32[128]{0:T(128)} %get-tuple-element.11) | copy-start | bytes 1540
  512.8 31.6 %copy-start.13 = (bf16[128,576]{0,1:T(8,128)(2,1)S(1)}, bf16[128,576]{0,1:T(8,128)(2,1)}, u32[]{:S(2)}) copy-start(bf16[128,576]{0,1:T(8,128)(2,1)} %copy-done.12) | copy-start | bytes 442372
  512.9 31.6 %copy-start.59 = (f32[128]{0:T(128)S(1)}, f32[128]{0:T(128)}, u32[]{:S(2)}) copy-start(f32[128]{0:T(128)} %copy-done.58) | copy-start | bytes 1540
  512.9 31.6 %copy-start.66 = (f32[128]{0:T(128)S(1)}, f32[128]{0:T(128)}, u32[]{:S(2)}) copy-start(f32[128]{0:T(128)} %get-tuple-element.42) | copy-start | bytes 1540
  557.2 24.9 %copy-start.17 = (bf16[128,576]{0,1:T(8,128)(2,1)S(1)}, bf16[128,576]{0,1:T(8,128)(2,1)}, u32[]{:S(2)}) copy-start(bf16[128,576]{0,1:T(8,128)(2,1)} %get-tuple-element.30) | copy-start | bytes 442372
  557.2 24.9 %copy-start.35 = (f32[576]{0:T(1024)S(1)}, f32[576]{0:T(1024)}, u32[]{:S(2)}) copy-start(f32[576]{0:T(1024)} %copy-done.34) | copy-start | bytes 6916
  557.3 24.9 %copy-start.47 = (f32[128]{0:T(128)S(1)}, f32[128]{0:T(128)}, u32[]{:S(2)}) copy-start(f32[128]{0:T(128)} %copy-done.45) | copy-start | bytes 1540
  557.3 24.9 %copy-start.62 = (f32[128]{0:T(128)S(1)}, f32[128]{0:T(128)}, u32[]{:S(2)}) copy-start(f32[128]{0:T(128)} %get-tuple-element.40) | copy-start | bytes 1540
  557.3 60.1 %copy-start.56 = (s32[128]{0:T(128)S(1)}, s32[128]{0:T(128)}, u32[]{:S(2)}) copy-start(s32[128]{0:T(128)} %get-tuple-element.35) | copy-start | bytes 1540
  559.6 22.6 %collective-permute-start.3 = (bf16[128,576]{0,1:T(8,128)(2,1)S(1)}, bf16[128,576]{0,1:T(8,128)(2,1)S(1)}, u32[]{:S(2)}, u32[]{:S(2)}) collective-permute-start(bf16[128,576]{0,1:T(8,128)(2,1)S(1)} %fusion.104), channel_id=1, source_target_pairs={{4,0},{8,4},{12,8},{16,12},{20,16},{24,20},{28,24},{5,1},{9,5},{13... | collective-permute-start | bytes 442376 | tf_op jit(solution)/shard_map/ppermute | solution.py:29
  (53 other events, 245.1 us)
Sparse Core Ops, SparseCore 0:
  12.9 79.1 all-reduce.17
  95.3 25.0 reduce-scatter.6
  122.8 67.0 all-reduce.15
  208.3 23.9 reduce-scatter.8
  245.2 59.4 all-reduce.23
  339.6 22.1 reduce-scatter.10
  364.7 25.4 reduce-scatter.12
  393.3 25.0 reduce-scatter.14
  420.9 53.0 all-reduce.21
  508.9 25.0 reduce-scatter.16
  557.3 60.0 all-reduce.19
